TPU v7x, 32 devices: a whole 2x2x4 slice. The times are simulated.
32 devices in a mesh: xy: 8 (over y, x, core), gz: 4 (over z).
Axes of the slice: x: 2, y: 2, z: 4, core: 2. Of those that a mesh axis runs over, the one named last changes fastest.
Arguments:
- velocity: float32 [3, 16, 256, 1024], P(None, 'gz', 'xy'), may hold values from -6 to 6
- magnetic: float32 [3, 8, 128, 512], P(None, 'gz', 'xy'), may hold values from -6 to 6
- slot_block_table: int32 [256], P('xy'), may hold values from 0 to 255, as said below
Outputs:
- updated_fine_velocity: float32 [3, 16, 256, 1024], P(None, 'gz', 'xy')
- magnetic_next: float32 [3, 8, 128, 512], P(None, 'gz', 'xy')
Inputs may be any that keep to these rules, and one draw needn't show every extreme that they name: `slot_block_table`: each block number appears in one slot; the 32 slots of one device along xy hold exactly 4 blocks of every block row.
All inputs are finite; a program needn't handle non-finite values.
Results may differ from a plain program's by a relative error of at most 0.00005.
Values sent between devices are 32-bit elements; how exact they have to be, the bound alone decides.
No kernel may reach another device: no remote copies, remote signals or barrier semaphores. Data moves between devices by JAX's collectives and lax.ppermute only.
A program may use at most 64 MiB of HBM per device.

v0:
```python
import jax
import jax.numpy as jnp
from jax import lax
from jax.sharding import PartitionSpec as P

BLOCK_EDGE = 32


def with_halo(value, sides, width):
    for axis, dim in sides:
        size, length = (lax.axis_size(axis), value.shape[dim])
        up = [(i, (i + 1) % size) for i in range(size)]
        down = [(j, i) for i, j in up]
        last = lax.slice_in_dim(value, length - width, length, axis=dim)
        first = lax.slice_in_dim(value, 0, width, axis=dim)
        before = lax.ppermute(last, axis, up)
        after = lax.ppermute(first, axis, down)
        value = jnp.concatenate([before, value, after], axis=dim)
    return value


def restrict(fine, blk):
    half_width = blk // 2
    s = fine.shape
    v = fine.reshape(s[0], s[1] // 2, 2, s[2], half_width, 2, half_width, 2)
    return (jnp.sum(v, axis=(2, 5, 7)) * 0.125).reshape(
        s[0], s[1] // 2, s[2], half_width * half_width
    )


def inner(padded):
    return padded[:, 1:-1, 1:-1]


def along_z(padded):
    return (padded[:, 2:, 1:-1] - padded[:, :-2, 1:-1]) * 0.5


def along_y(padded):
    return (padded[:, 1:-1, 2:] - padded[:, 1:-1, :-2]) * 0.5


def along_x(padded):
    middle = inner(padded)
    return (jnp.roll(middle, -1, 3) - jnp.roll(middle, 1, 3)) * 0.5


def curl_padded(padded):
    dzv = along_z(padded)
    dyv = along_y(padded)
    dxv = along_x(padded)
    return jnp.stack([dyv[2] - dzv[1], dzv[0] - dxv[2], dxv[1] - dyv[0]])


def cross(a, b):
    return jnp.stack(
        [a[1] * b[2] - a[2] * b[1], a[2] * b[0] - a[0] * b[2], a[0] * b[1] - a[1] * b[0]]
    )


def laplace_padded(padded):
    middle = inner(padded)
    total = padded[:, 2:, 1:-1] + padded[:, :-2, 1:-1] + padded[:, 1:-1, 2:] + padded[:, 1:-1, :-2]
    return total + jnp.roll(middle, 1, 3) + jnp.roll(middle, -1, 3) - 6.0 * middle


def split_into_tiles(magnetic_state, coarse_depth_index, half_width, slot_count):
    return (
        magnetic_state.reshape(
            magnetic_state.shape[0], coarse_depth_index, half_width, slot_count, half_width
        )
        .transpose(0, 1, 3, 2, 4)
        .reshape(magnetic_state.shape[0], coarse_depth_index, slot_count, half_width * half_width)
    )


def assemble_from_tiles(tile_stack, coarse_depth_index, half_width, slot_count):
    return (
        tile_stack.reshape(
            tile_stack.shape[0], coarse_depth_index, slot_count, half_width, half_width
        )
        .transpose(0, 1, 3, 2, 4)
        .reshape(tile_stack.shape[0], coarse_depth_index, half_width, slot_count * half_width)
    )


def body(velocity, magnetic, slot_block_table):
    half_width = BLOCK_EDGE // 2
    slot_count = velocity.shape[2]
    coarse_depth_index = velocity.shape[1] // 2
    column_indices = slot_block_table % slot_count
    sorted_positions = jnp.argsort(slot_block_table)
    dispatched_columns = column_indices[sorted_positions].reshape(1, 1, slot_count, 1)
    ordered = velocity[:, :, sorted_positions]
    got, received_columns = (
        lax.all_to_all(
            restrict(ordered, BLOCK_EDGE), "xy", split_axis=2, concat_axis=2, tiled=True
        ),
        lax.all_to_all(dispatched_columns, "xy", split_axis=2, concat_axis=2, tiled=True),
    )
    column_listing = received_columns.reshape(slot_count)
    grouped_by_column = got[:, :, jnp.argsort(column_listing)]
    coarse_flow_field = assemble_from_tiles(
        grouped_by_column, coarse_depth_index, half_width, slot_count
    )
    emf = cross(coarse_flow_field, magnetic)
    stacked = jnp.concatenate([magnetic, emf], axis=0)
    padded = with_halo(stacked, (("xy", 2), ("gz", 1)), 1)
    field_pad = padded[0:3]
    current = curl_padded(field_pad)
    magnetic_next = magnetic + 0.1 * (curl_padded(padded[3:6]) + 0.5 * laplace_padded(field_pad))
    lorentz_force = cross(current, magnetic)
    returned_back_tiles = split_into_tiles(
        lorentz_force, coarse_depth_index, half_width, slot_count
    )[:, :, column_listing]
    returned = lax.all_to_all(returned_back_tiles, "xy", split_axis=2, concat_axis=2, tiled=True)
    blocks_per_slot = returned[:, :, jnp.argsort(sorted_positions)]
    widened_tiles = jnp.broadcast_to(
        blocks_per_slot.reshape(3, coarse_depth_index, 1, slot_count, half_width, 1, half_width, 1),
        (3, coarse_depth_index, 2, slot_count, half_width, 2, half_width, 2),
    )
    updated_fine_velocity = velocity + 0.1 * widened_tiles.reshape(
        3, coarse_depth_index * 2, slot_count, BLOCK_EDGE * BLOCK_EDGE
    )
    return (updated_fine_velocity, magnetic_next)


def solution(mesh):
    return jax.shard_map(
        body,
        mesh=mesh,
        in_specs=(P(None, "gz", "xy", None), P(None, "gz", "xy", None), P("xy")),
        out_specs=(P(None, "gz", "xy", None), P(None, "gz", "xy", None)),
        check_vma=False,
    )
```

profile of v0, /device:TPU:0, one launch (start us, length us, event | category | flops | bytes accessed | tf_op | source)
XLA Modules:
  0.0 104.9 jit_solution(8437130082161293835)
XLA Ops:
  1.4 2.3 %sort.45 = (s32[32]{0:T(128)}, s32[32]{0:T(128)S(1)}) sort(s32[32]{0:T(128)} %param.5, s32[32]{0:T(128)S(1)} %iota.10), dimensions={0}, to_apply=%region_0.1 | sort | flops 160 | bytes 512 | tf_op jit(solution)/shard_map/jit(argsort)/sort | solution.py:92
  5.7 5.2 %all-to-all-start.1 = ((s32[1,1,32,1]{3,1,0,2:T(1,128)}), s32[1,1,32,1]{3,1,0,2:T(1,128)S(1)}, u32[]{:S(2)}, u32[]{:S(2)}) async-start(s32[1,1,32,1]{3,1,0,2:T(1,128)} %copy.33), calls=%async_computation.1 | async-start | bytes 32768 | tf_op jit(solution)/shard_map/all_to_all | solution.py:99
  10.9 1.5 %fusion.14 = (f32[3,2,16,1]{3,2,1,0:T(8,128)}, f32[3,2,16,1]{3,2,1,0:T(8,128)}) fusion(f32[3,2,16,512]{3,2,1,0:T(8,128)} %param.4), kind=kLoop, calls=%fused_computation.82 | loop fusion | bytes 1536 | tf_op jit(solution)/shard_map/jit(_roll_static)/slice | solution.py:45
  13.6 3.0 %gather_fusion = f32[32,3,4,1024]{3,0,2,1:T(8,128)S(1)} fusion(f32[3,4,32,1024]{3,2,1,0:T(8,128)S(1)} %copy-done, s32[1024]{0:T(1024)} %copy-done.18), kind=kCustom, calls=%fused_computation | custom fusion | bytes 3145856 | tf_op jit(solution)/shard_map/gather | solution.py:94
  16.5 4.0 %copy.43 = f32[3,4,32,1024]{2,3,1,0:T(8,128)} copy(f32[3,4,32,1024]{3,2,1,0:T(8,128)S(1)} %copy-done) | data formatting | bytes 3145728 | tf_op args[0]
  20.5 2.3 %sort.47 = (s32[32]{0:T(128)}, s32[32]{0:T(128)S(1)}) sort(s32[32]{0:T(128)} %copy-done.19, s32[32]{0:T(128)S(1)} %iota.12), dimensions={0}, to_apply=%region_3.4 | sort | flops 160 | bytes 512 | tf_op jit(solution)/shard_map/jit(argsort)/sort | solution.py:117
  23.4 4.0 %copy.31 = f32[3,4,32,1024]{2,3,1,0:T(8,128)} copy(f32[3,4,32,1024]{3,2,1,0:T(8,128)S(1)} %bitcast.34) | data formatting | bytes 3145728 | tf_op jit(solution)/shard_map/gather | solution.py:94
  27.3 7.3 %reduce_sum.9 = f32[3,2,32,16,16]{2,4,3,1,0:T(8,128)S(1)} reduce(f32[3,2,2,32,16,2,16,2]{3,7,6,5,4,2,1,0:T(2,128)} %bitcast.32, f32[]{:T(128)} %constant.10.clone.1), dimensions={2,5,7}, to_apply=%region_1.2 | reduce | flops 344064 | bytes 1769476 | tf_op jit(solution)/shard_map/reduce_sum | solution.py:26
  36.5 4.2 %all-to-all-start = ((f32[3,2,32,256]{3,1,0,2:T(2,128)}), f32[3,2,32,256]{3,1,0,2:T(2,128)S(1)}, u32[]{:S(2)}, u32[]{:S(2)}) async-start(f32[3,2,32,256]{3,1,0,2:T(2,128)} %copy.32), calls=%async_computation | async-start | bytes 393216 | tf_op jit(solution)/shard_map/all_to_all | solution.py:96
  41.4 1.6 %sort.46 = (s32[32]{0:T(128)}, s32[32]{0:T(128)S(1)}) sort(s32[32]{0:T(128)S(1)} %reduce, s32[32]{0:T(128)S(1)} %iota.11), dimensions={0}, to_apply=%region_2.3 | sort | flops 160 | bytes 512 | tf_op jit(solution)/shard_map/jit(argsort)/sort | solution.py:102
  43.0 3.9 %all-to-all-done = f32[3,2,32,256]{3,1,0,2:T(2,128)S(1)} async-done(((f32[3,2,32,256]{3,1,0,2:T(2,128)}), f32[3,2,32,256]{3,1,0,2:T(2,128)S(1)}, u32[]{:S(2)}, u32[]{:S(2)}) %all-to-all-start) | async-done | bytes 196640 | tf_op jit(solution)/shard_map/all_to_all | solution.py:96
  49.8 2.6 %collective-permute-start.1 = (f32[6,2,1,512]{3,2,1,0:T(1,128)S(1)}, f32[6,2,1,512]{3,2,1,0:T(1,128)S(1)}, u32[]{:S(2)}, u32[]{:S(2)}) collective-permute-start(f32[6,2,1,512]{3,2,1,0:T(1,128)S(1)} %get-tuple-element.23), channel_id=1, source_target_pairs={{4,0},{8,4},{12,8},{16,12},{20,16},{24,20},{28,24},{0,28},{5,1},{9... | collective-permute-start | bytes 73736 | tf_op jit(solution)/shard_map/ppermute | solution.py:17
  52.4 1.7 %collective-permute-done = f32[6,2,1,512]{3,2,1,0:T(1,128)S(1)} collective-permute-done((f32[6,2,1,512]{3,2,1,0:T(1,128)S(1)}, f32[6,2,1,512]{3,2,1,0:T(1,128)S(1)}, u32[]{:S(2)}, u32[]{:S(2)}) %collective-permute-start) | collective-permute-done | bytes 24608 | tf_op jit(solution)/shard_map/ppermute | solution.py:16
  54.3 1.6 %collective-permute-start.3 = (f32[6,1,18,512]{3,2,1,0:T(8,128)S(1)}, f32[6,1,18,512]{3,2,1,0:T(8,128)S(1)}, u32[]{:S(2)}, u32[]{:S(2)}) collective-permute-start(f32[6,1,18,512]{3,2,1,0:T(8,128)S(1)} %get-tuple-element.20), channel_id=1, source_target_pairs={{0,1},{1,2},{2,3},{3,0},{4,5},{5,6},{6,7},{7,4},{8,9},{9,10},{10,1... | collective-permute-start | bytes 663560 | tf_op jit(solution)/shard_map/ppermute | solution.py:16
  55.9 2.3 %collective-permute-start.2 = (f32[6,1,18,512]{3,2,1,0:T(8,128)S(1)}, f32[6,1,18,512]{3,2,1,0:T(8,128)S(1)}, u32[]{:S(2)}, u32[]{:S(2)}) collective-permute-start(f32[6,1,18,512]{3,2,1,0:T(8,128)S(1)} %get-tuple-element.21), channel_id=1, source_target_pairs={{1,0},{2,1},{3,2},{0,3},{5,4},{6,5},{7,6},{4,7},{9,8},{10,9},{11,1... | collective-permute-start | bytes 663560 | tf_op jit(solution)/shard_map/ppermute | solution.py:17
  59.0 7.1 %collective-permute-done.3 = f32[6,1,18,512]{3,2,1,0:T(8,128)S(1)} collective-permute-done((f32[6,1,18,512]{3,2,1,0:T(8,128)S(1)}, f32[6,1,18,512]{3,2,1,0:T(8,128)S(1)}, u32[]{:S(2)}, u32[]{:S(2)}) %collective-permute-start.3) | collective-permute-done | bytes 221216 | tf_op jit(solution)/shard_map/ppermute | solution.py:16
  66.0 4.7 %collective-permute-done.2 = f32[6,1,18,512]{3,2,1,0:T(8,128)S(1)} collective-permute-done((f32[6,1,18,512]{3,2,1,0:T(8,128)S(1)}, f32[6,1,18,512]{3,2,1,0:T(8,128)S(1)}, u32[]{:S(2)}, u32[]{:S(2)}) %collective-permute-start.2) | collective-permute-done | bytes 221216 | tf_op jit(solution)/shard_map/ppermute | solution.py:17
  75.3 1.4 %maximum_bitcast_fusion = f32[3,2,32,16,16]{4,2,3,1,0:T(8,128)S(1)} fusion(f32[1,2,16,32,16]{4,3,2,1,0:T(8,128)} %stack.23, f32[1,2,16,32,16]{4,3,2,1,0:T(8,128)} %stack.22, f32[1,2,16,32,16]{4,3,2,1,0:T(8,128)S(1)} %stack.10), kind=kLoop, calls=%fused_computation.5 | loop fusion | flops 98304 | bytes 393216 | tf_op jit(solution)/shard_map/transpose | solution.py:72
  77.5 1.5 %gather_fusion.3 = f32[32,3,2,256]{3,2,1,0:T(2,128)} fusion(f32[3,2,32,256]{3,1,2,0:T(2,128)S(1)} %copy.40, s32[1024]{0:T(1024)S(1)} %pad_clamp_fusion.1), kind=kCustom, calls=%fused_computation.3 | custom fusion | bytes 393344 | tf_op jit(solution)/shard_map/gather | solution.py:113
  78.9 3.4 %all-to-all-start.2 = ((f32[3,2,32,256]{3,1,0,2:T(2,128)}), f32[3,2,32,256]{3,1,0,2:T(2,128)S(1)}, u32[]{:S(2)}, u32[]{:S(2)}) async-start(f32[3,2,32,256]{3,1,0,2:T(2,128)} %bitcast.11), calls=%async_computation.2 | async-start | bytes 393216 | tf_op jit(solution)/shard_map/all_to_all | solution.py:116
  83.5 5.0 %all-to-all-done.2 = f32[3,2,32,256]{3,1,0,2:T(2,128)S(1)} async-done(((f32[3,2,32,256]{3,1,0,2:T(2,128)}), f32[3,2,32,256]{3,1,0,2:T(2,128)S(1)}, u32[]{:S(2)}, u32[]{:S(2)}) %all-to-all-start.2) | async-done | bytes 196640 | tf_op jit(solution)/shard_map/all_to_all | solution.py:116
  89.8 3.2 %broadcast_in_dim.19 = f32[3,2,2,32,16,2,16,2]{3,7,6,5,4,2,1,0:T(2,128)S(1)} broadcast(f32[3,2,32,16,16]{2,4,3,1,0:T(8,128)S(1)} %bitcast.35), dimensions={0,1,3,4,6} | broadcast | bytes 1769472 | tf_op jit(solution)/shard_map/broadcast_in_dim | solution.py:118
  93.0 6.3 %add.55 = f32[3,4,32,1024]{2,3,1,0:T(8,128)} add(f32[3,4,32,1024]{2,3,1,0:T(8,128)} %copy.43, f32[3,4,32,1024]{2,3,1,0:T(8,128)S(1)} %bitcast.33) | non-fusion elementwise | flops 393216 | bytes 4718592 | tf_op jit(solution)/shard_map/add | solution.py:122
  99.3 5.5 %copy.44 = f32[3,4,32,1024]{3,2,1,0:T(8,128)} copy(f32[3,4,32,1024]{2,3,1,0:T(8,128)} %add.55) | data formatting | bytes 3145728
  (95 shorter events, 18.4 us)
Async XLA Ops:
  0.6 12.9 %copy-start = (f32[3,4,32,1024]{3,2,1,0:T(8,128)S(1)}, f32[3,4,32,1024]{3,2,1,0:T(8,128)}, u32[]{:S(2)}) copy-start(f32[3,4,32,1024]{3,2,1,0:T(8,128)} %param.3) | copy-start | bytes 4718596
  4.3 8.1 %copy-start.18 = (s32[1024]{0:T(1024)}, s32[1024]{0:T(1024)S(1)}, u32[]{:S(2)}) copy-start(s32[1024]{0:T(1024)S(1)} %pad_clamp_fusion.3) | copy-start | bytes 12292
  5.7 30.8 %all-to-all-start.1 = ((s32[1,1,32,1]{3,1,0,2:T(1,128)}), s32[1,1,32,1]{3,1,0,2:T(1,128)S(1)}, u32[]{:S(2)}, u32[]{:S(2)}) async-start(s32[1,1,32,1]{3,1,0,2:T(1,128)} %copy.33), calls=%async_computation.1 | async-start | bytes 32768 | tf_op jit(solution)/shard_map/all_to_all | solution.py:99
  13.6 21.2 %copy-start.2 = (f32[3,2,16,511]{3,2,1,0:T(8,128)}, f32[3,2,16,511]{3,2,1,0:T(8,128)S(1)}, u32[]{:S(2)}) copy-start(f32[3,2,16,511]{3,2,1,0:T(8,128)S(1)} %get-tuple-element.37) | copy-start | bytes 588676
  36.5 10.4 %all-to-all-start = ((f32[3,2,32,256]{3,1,0,2:T(2,128)}), f32[3,2,32,256]{3,1,0,2:T(2,128)S(1)}, u32[]{:S(2)}, u32[]{:S(2)}) async-start(f32[3,2,32,256]{3,1,0,2:T(2,128)} %copy.32), calls=%async_computation | async-start | bytes 393216 | tf_op jit(solution)/shard_map/all_to_all | solution.py:96
  48.3 1.3 %copy-start.1 = (f32[3,2,16,512]{3,2,1,0:T(8,128)S(1)}, f32[3,2,16,512]{3,2,1,0:T(8,128)}, u32[]{:S(2)}) copy-start(f32[3,2,16,512]{3,2,1,0:T(8,128)} %param.4) | copy-start | bytes 589828
  49.7 4.4 %collective-permute-start = (f32[6,2,1,512]{3,2,1,0:T(1,128)S(1)}, f32[6,2,1,512]{3,2,1,0:T(1,128)S(1)}, u32[]{:S(2)}, u32[]{:S(2)}) collective-permute-start(f32[6,2,1,512]{3,2,1,0:T(1,128)S(1)} %get-tuple-element.22), channel_id=1, source_target_pairs={{0,4},{4,8},{8,12},{12,16},{16,20},{20,24},{24,28},{28,0},{1,5},{5... | collective-permute-start | bytes 73736 | tf_op jit(solution)/shard_map/ppermute | solution.py:16
  49.8 4.4 %collective-permute-start.1 = (f32[6,2,1,512]{3,2,1,0:T(1,128)S(1)}, f32[6,2,1,512]{3,2,1,0:T(1,128)S(1)}, u32[]{:S(2)}, u32[]{:S(2)}) collective-permute-start(f32[6,2,1,512]{3,2,1,0:T(1,128)S(1)} %get-tuple-element.23), channel_id=1, source_target_pairs={{4,0},{8,4},{12,8},{16,12},{20,16},{24,20},{28,24},{0,28},{5,1},{9... | collective-permute-start | bytes 73736 | tf_op jit(solution)/shard_map/ppermute | solution.py:17
  54.1 18.8 %copy-start.4 = (f32[6,2,1,512]{3,2,1,0:T(1,128)}, f32[6,2,1,512]{3,2,1,0:T(1,128)S(1)}, u32[]{:S(2)}) copy-start(f32[6,2,1,512]{3,2,1,0:T(1,128)S(1)} %collective-permute-done) | copy-start | bytes 73732
  54.1 18.8 %copy-start.6 = (f32[6,2,1,512]{3,2,1,0:T(1,128)}, f32[6,2,1,512]{3,2,1,0:T(1,128)S(1)}, u32[]{:S(2)}) copy-start(f32[6,2,1,512]{3,2,1,0:T(1,128)S(1)} %collective-permute-done.1) | copy-start | bytes 73732
  54.3 11.8 %collective-permute-start.3 = (f32[6,1,18,512]{3,2,1,0:T(8,128)S(1)}, f32[6,1,18,512]{3,2,1,0:T(8,128)S(1)}, u32[]{:S(2)}, u32[]{:S(2)}) collective-permute-start(f32[6,1,18,512]{3,2,1,0:T(8,128)S(1)} %get-tuple-element.20), channel_id=1, source_target_pairs={{0,1},{1,2},{2,3},{3,0},{4,5},{5,6},{6,7},{7,4},{8,9},{9,10},{10,1... | collective-permute-start | bytes 663560 | tf_op jit(solution)/shard_map/ppermute | solution.py:16
  55.9 14.8 %collective-permute-start.2 = (f32[6,1,18,512]{3,2,1,0:T(8,128)S(1)}, f32[6,1,18,512]{3,2,1,0:T(8,128)S(1)}, u32[]{:S(2)}, u32[]{:S(2)}) collective-permute-start(f32[6,1,18,512]{3,2,1,0:T(8,128)S(1)} %get-tuple-element.21), channel_id=1, source_target_pairs={{1,0},{2,1},{3,2},{0,3},{5,4},{6,5},{7,6},{4,7},{9,8},{10,9},{11,1... | collective-permute-start | bytes 663560 | tf_op jit(solution)/shard_map/ppermute | solution.py:17
  77.1 5.2 %copy-start.8 = (f32[3,2,16,511]{3,2,1,0:T(8,128)S(1)}, f32[3,2,16,511]{3,2,1,0:T(8,128)}, u32[]{:S(2)}) copy-start(f32[3,2,16,511]{3,2,1,0:T(8,128)} %get-tuple-element.34) | copy-start | bytes 588676
  77.1 5.2 %copy-start.9 = (f32[3,2,16,511]{3,2,1,0:T(8,128)S(1)}, f32[3,2,16,511]{3,2,1,0:T(8,128)}, u32[]{:S(2)}) copy-start(f32[3,2,16,511]{3,2,1,0:T(8,128)} %get-tuple-element.35) | copy-start | bytes 588676
  77.1 5.2 %copy-start.16 = (f32[3,2,16,1]{3,2,1,0:T(8,128)S(1)}, f32[3,2,16,1]{3,2,1,0:T(8,128)}, u32[]{:S(2)}) copy-start(f32[3,2,16,1]{3,2,1,0:T(8,128)} %get-tuple-element.32) | copy-start | bytes 1156
  77.1 5.2 %copy-start.17 = (f32[3,2,16,1]{3,2,1,0:T(8,128)S(1)}, f32[3,2,16,1]{3,2,1,0:T(8,128)}, u32[]{:S(2)}) copy-start(f32[3,2,16,1]{3,2,1,0:T(8,128)} %get-tuple-element.33) | copy-start | bytes 1156
  77.2 5.4 %copy-start.10 = (f32[3,2,16,512]{3,2,1,0:T(8,128)S(1)}, f32[3,2,16,512]{3,2,1,0:T(8,128)}, u32[]{:S(2)}) copy-start(f32[3,2,16,512]{3,2,1,0:T(8,128)} %fusion.3) | copy-start | bytes 589828
  77.2 5.4 %copy-start.11 = (f32[3,2,16,512]{3,2,1,0:T(8,128)S(1)}, f32[3,2,16,512]{3,2,1,0:T(8,128)}, u32[]{:S(2)}) copy-start(f32[3,2,16,512]{3,2,1,0:T(8,128)} %get-tuple-element.30) | copy-start | bytes 589828
  77.2 5.4 %copy-start.3 = (f32[3,2,16,511]{3,2,1,0:T(8,128)S(1)}, f32[3,2,16,511]{3,2,1,0:T(8,128)}, u32[]{:S(2)}) copy-start(f32[3,2,16,511]{3,2,1,0:T(8,128)} %copy-done.2) | copy-start | bytes 588676
  77.2 5.4 %copy-start.5 = (f32[6,2,1,512]{3,2,1,0:T(1,128)S(1)}, f32[6,2,1,512]{3,2,1,0:T(1,128)}, u32[]{:S(2)}) copy-start(f32[6,2,1,512]{3,2,1,0:T(1,128)} %copy-done.4) | copy-start | bytes 73732
  77.2 5.4 %copy-start.7 = (f32[6,2,1,512]{3,2,1,0:T(1,128)S(1)}, f32[6,2,1,512]{3,2,1,0:T(1,128)}, u32[]{:S(2)}) copy-start(f32[6,2,1,512]{3,2,1,0:T(1,128)} %copy-done.6) | copy-start | bytes 73732
  77.2 5.4 %copy-start.13 = (f32[3,2,16,1]{3,2,1,0:T(8,128)S(1)}, f32[3,2,16,1]{3,2,1,0:T(8,128)}, u32[]{:S(2)}) copy-start(f32[3,2,16,1]{3,2,1,0:T(8,128)} %get-tuple-element.38) | copy-start | bytes 1156
  77.2 5.4 %copy-start.15 = (f32[3,2,16,1]{3,2,1,0:T(8,128)S(1)}, f32[3,2,16,1]{3,2,1,0:T(8,128)}, u32[]{:S(2)}) copy-start(f32[3,2,16,1]{3,2,1,0:T(8,128)} %get-tuple-element.39) | copy-start | bytes 1156
  78.9 9.5 %all-to-all-start.2 = ((f32[3,2,32,256]{3,1,0,2:T(2,128)}), f32[3,2,32,256]{3,1,0,2:T(2,128)S(1)}, u32[]{:S(2)}, u32[]{:S(2)}) async-start(f32[3,2,32,256]{3,1,0,2:T(2,128)} %bitcast.11), calls=%async_computation.2 | async-start | bytes 393216 | tf_op jit(solution)/shard_map/all_to_all | solution.py:116
  (3 other events, 2.2 us)
where the time goes:
time: 106 us; the launch traced here: 105 us
  local copies, waits for them, and re-layouts  35.8 us (34%)
  other arithmetic  26.2 us (25%)
  waiting for transfers between devices  22.3 us (21%)
  starting transfers between devices  19.4 us (18%)
  between operations  1.12 us (1%)
    unnamed x42, local copies, waits for them, and re-layouts  10.9 us
    ppermute x2, waiting for transfers between devices, with_halo(): before = lax.ppermute(last, axis, up)  8.8 us
    reduce_sum x1, other arithmetic, restrict(): jnp.sum(v, axis=(2, 5, 7)) * 0.125  7.27 us
    gather x2, local copies, waits for them, and re-layouts, body(): ordered = velocity[:, :, sorted_positions]  6.93 us
    add x1, other arithmetic, body(): velocity + 0.1 * widened_tiles.reshape(3, coarse_depth_index * 2, slot_co...  6.28 us
    all_to_all x1, starting transfers between devices, body(): lax.all_to_all(dispatched_columns, 'xy', split_axis=2, concat_axis=2, til...  5.2 us
    all_to_all x1, waiting for transfers between devices, body(): lax.all_to_all(returned_back_tiles, 'xy', split_axis=2, concat_axis=2, ti...  4.99 us
    ppermute x2, starting transfers between devices, with_halo(): after = lax.ppermute(first, axis, down)  4.9 us
  transfers between devices with their start and end apart: 7, of which 5 were waited for; matrix products, arithmetic and copies ran while one was open for 28% of the time, Pallas kernels for 0%

commit v1 on v0

--- a/solution.py
+++ b/solution.py
@@ -4,6 +4,28 @@
 from jax.sharding import PartitionSpec as P
 
 BLOCK_EDGE = 32
+
+
+def cut_along(value, dim, count):
+    before, after = (value.shape[:dim], value.shape[dim + 1 :])
+    return jnp.moveaxis(value.reshape(*before, count, -1, *after), dim, 0)
+
+
+def joined_along(blocks, dim):
+    blocks = jnp.moveaxis(blocks, 0, dim)
+    lengths = blocks.shape
+    return blocks.reshape(*lengths[:dim], lengths[dim] * lengths[dim + 1], *lengths[dim + 2 :])
+
+
+def swapped_with_each(x, axis, split_dim, concat_dim):
+    size, place = (lax.axis_size(axis), lax.axis_index(axis))
+    pieces = cut_along(x, split_dim, size)
+    outs = [pieces[place]]
+    for turn in range(1, size):
+        sent = pieces[place ^ turn]
+        outs.append(lax.ppermute(sent, axis, [(i, i ^ turn) for i in range(size)]))
+    pieces = jnp.stack(outs)[place ^ jnp.arange(size)]
+    return joined_along(pieces, concat_dim)
 
 
 def with_halo(value, sides, width):
@@ -96,7 +118,7 @@
         lax.all_to_all(
             restrict(ordered, BLOCK_EDGE), "xy", split_axis=2, concat_axis=2, tiled=True
         ),
-        lax.all_to_all(dispatched_columns, "xy", split_axis=2, concat_axis=2, tiled=True),
+        swapped_with_each(dispatched_columns, "xy", 2, 2),
     )
     column_listing = received_columns.reshape(slot_count)
     grouped_by_column = got[:, :, jnp.argsort(column_listing)]

time: 106 us -> 102 us (0.962)
  local copies, waits for them, and re-layouts: 35.8 us -> 32.3 us
  starting transfers between devices: 19.4 us -> 22.2 us
  other arithmetic: 26.2 us -> 24.3 us
  waiting for transfers between devices: 22.3 us -> 21.1 us
    ppermute x0 -> x7, starting transfers between devices: none -> 8.84 us  [swapped_with_each(): outs.append(lax.ppermute(sent, axis, [(i, i ^ turn) for i in range(size)]))]
    all_to_all x1 -> x0, starting transfers between devices: 5.2 us -> none  [body(): lax.all_to_all(dispatched_columns, 'xy', split_axis=2, concat_axis=2, til...]
    all_to_all x1, waiting for transfers between devices: 3.9 us -> 0.01 us  [body(): lax.all_to_all(restrict(ordered, BLOCK_EDGE), 'xy', split_axis=2, concat_...]
    slice x4, local copies, waits for them, and re-layouts: 4.15 us -> 1.69 us  [along_x(): return (jnp.roll(middle, -1, 3) - jnp.roll(middle, 1, 3)) * 0.5]
    ppermute x0 -> x7, waiting for transfers between devices: none -> 1.64 us  [swapped_with_each(): outs.append(lax.ppermute(sent, axis, [(i, i ^ turn) for i in range(size)]))]
    ppermute x2, waiting for transfers between devices: 4.65 us -> 6.09 us  [with_halo(): after = lax.ppermute(first, axis, down)]
    unnamed x42 -> x38, local copies, waits for them, and re-layouts: 10.9 us -> 9.62 us
  transfers between devices with their start and end apart: 7 -> 13, of which waited for: 5 -> 5; matrix products, arithmetic and copies ran while one was open for 28% -> 25% of each run, Pallas kernels for 0% -> 0%
where the time goes in v1:
time: 102 us; the launch traced here: 101 us
  local copies, waits for them, and re-layouts  32.3 us (32%)
  other arithmetic  24.3 us (24%)
  starting transfers between devices  22.2 us (22%)
  waiting for transfers between devices  21.1 us (21%)
  between operations  1.21 us (1%)
    unnamed x38, local copies, waits for them, and re-layouts  9.62 us
    ppermute x7, starting transfers between devices, swapped_with_each(): outs.append(lax.ppermute(sent, axis, [(i, i ^ turn) for i in range(size)]))  8.84 us
    ppermute x2, waiting for transfers between devices, with_halo(): before = lax.ppermute(last, axis, up)  8.4 us
    reduce_sum x1, other arithmetic, restrict(): jnp.sum(v, axis=(2, 5, 7)) * 0.125  7.27 us
    gather x2, local copies, waits for them, and re-layouts, body(): ordered = velocity[:, :, sorted_positions]  7.18 us
    add x1, other arithmetic, body(): velocity + 0.1 * widened_tiles.reshape(3, coarse_depth_index * 2, slot_co...  6.3 us
    ppermute x2, waiting for transfers between devices, with_halo(): after = lax.ppermute(first, axis, down)  6.09 us
    all_to_all x1, waiting for transfers between devices, body(): lax.all_to_all(returned_back_tiles, 'xy', split_axis=2, concat_axis=2, ti...  4.99 us
  transfers between devices with their start and end apart: 13, of which 5 were waited for; matrix products, arithmetic and copies ran while one was open for 25% of the time, Pallas kernels for 0%

profile of v1, /device:TPU:0, one launch (start us, length us, event | category | flops | bytes accessed | tf_op | source)
XLA Modules:
  0.0 101.1 jit_solution(16201033667573360222)
XLA Ops:
  0.7 2.3 %sort.45 = (s32[32]{0:T(128)}, s32[32]{0:T(128)S(1)}) sort(s32[32]{0:T(128)} %param.5, s32[32]{0:T(128)S(1)} %iota.14), dimensions={0}, to_apply=%region_0.1 | sort | flops 160 | bytes 512 | tf_op jit(solution)/shard_map/jit(argsort)/sort | solution.py:114
  4.4 3.4 %collective-permute-start.6 = (s32[1,1,4,1]{2,3,1,0:T(1,128)S(1)}, s32[1,1,4,1]{2,3,1,0:T(1,128)S(1)}, u32[]{:S(2)}, u32[]{:S(2)}) collective-permute-start(s32[1,1,4,1]{2,3,1,0:T(1,128)S(1)} %get-tuple-element.38), channel_id=1, source_target_pairs={{0,28},{4,24},{8,20},{12,16},{16,12},{20,8},{24,4},{28,0},{1,29},{... | collective-permute-start | bytes 56 | tf_op jit(solution)/shard_map/ppermute | solution.py:26
  11.3 3.2 %gather_fusion = f32[32,3,4,1024]{3,0,2,1:T(8,128)S(1)} fusion(f32[3,4,32,1024]{3,2,1,0:T(8,128)} %param.3, s32[1024]{0:T(1024)S(1)} %pad_clamp_fusion.4), kind=kCustom, calls=%fused_computation | custom fusion | bytes 3145856 | tf_op jit(solution)/shard_map/gather | solution.py:116
  14.4 4.0 %copy.35 = f32[3,4,32,1024]{2,3,1,0:T(8,128)} copy(f32[3,4,32,1024]{3,2,1,0:T(8,128)S(1)} %bitcast.69) | data formatting | bytes 3145728 | tf_op jit(solution)/shard_map/gather | solution.py:116
  18.5 7.3 %reduce_sum.9 = f32[3,2,32,16,16]{2,4,3,1,0:T(8,128)S(1)} reduce(f32[3,2,2,32,16,2,16,2]{3,7,6,5,4,2,1,0:T(2,128)} %bitcast.67, f32[]{:T(128)} %constant.20.clone.1), dimensions={2,5,7}, to_apply=%region_1.2 | reduce | flops 344064 | bytes 1769476 | tf_op jit(solution)/shard_map/reduce_sum | solution.py:48
  26.8 3.4 %all-to-all-start = ((f32[3,2,32,256]{3,1,0,2:T(2,128)}), f32[3,2,32,256]{3,1,0,2:T(2,128)S(1)}, u32[]{:S(2)}, u32[]{:S(2)}) async-start(f32[3,2,32,256]{3,1,0,2:T(2,128)} %copy.36), calls=%async_computation | async-start | bytes 393216 | tf_op jit(solution)/shard_map/all_to_all | solution.py:118
  30.4 4.0 %copy.55 = f32[3,4,32,1024]{2,3,1,0:T(8,128)} copy(f32[3,4,32,1024]{3,2,1,0:T(8,128)S(1)} %copy-done) | data formatting | bytes 3145728 | tf_op args[0]
  34.4 1.6 %sort.47 = (s32[32]{0:T(128)}, s32[32]{0:T(128)S(1)}) sort(s32[32]{0:T(128)S(1)} %get-tuple-element.5, s32[32]{0:T(128)S(1)} %iota.17), dimensions={0}, to_apply=%region_3.4 | sort | flops 160 | bytes 512 | tf_op jit(solution)/shard_map/jit(argsort)/sort | solution.py:139
  36.2 2.0 %collective-permute-start.1 = (s32[1,1,4,1]{2,3,1,0:T(1,128)S(1)}, s32[1,1,4,1]{2,3,1,0:T(1,128)S(1)}, u32[]{:S(2)}, u32[]{:S(2)}) collective-permute-start(s32[1,1,4,1]{2,3,1,0:T(1,128)S(1)} %get-tuple-element.43), channel_id=1, source_target_pairs={{0,8},{4,12},{8,0},{12,4},{16,24},{20,28},{24,16},{28,20},{1,9},{5... | collective-permute-start | bytes 56 | tf_op jit(solution)/shard_map/ppermute | solution.py:26
  38.2 1.6 %collective-permute-done.1 = s32[1,1,4,1]{2,3,1,0:T(1,128)S(1)} collective-permute-done((s32[1,1,4,1]{2,3,1,0:T(1,128)S(1)}, s32[1,1,4,1]{2,3,1,0:T(1,128)S(1)}, u32[]{:S(2)}, u32[]{:S(2)}) %collective-permute-start.1) | collective-permute-done | bytes 48 | tf_op jit(solution)/shard_map/ppermute | solution.py:26
  40.6 1.6 %sort.46 = (s32[32]{0:T(128)}, s32[32]{0:T(128)S(1)}) sort(s32[32]{0:T(128)S(1)} %reshape_reshape_transpose.5, s32[32]{0:T(128)S(1)} %iota.16), dimensions={0}, to_apply=%region_2.3 | sort | flops 160 | bytes 512 | tf_op jit(solution)/shard_map/jit(argsort)/sort | solution.py:124
  45.1 2.6 %collective-permute-start.8 = (f32[6,2,1,512]{3,2,1,0:T(1,128)S(1)}, f32[6,2,1,512]{3,2,1,0:T(1,128)S(1)}, u32[]{:S(2)}, u32[]{:S(2)}) collective-permute-start(f32[6,2,1,512]{3,2,1,0:T(1,128)S(1)} %get-tuple-element.21), channel_id=1, source_target_pairs={{4,0},{8,4},{12,8},{16,12},{20,16},{24,20},{28,24},{0,28},{5,1},{9... | collective-permute-start | bytes 73736 | tf_op jit(solution)/shard_map/ppermute | solution.py:39
  47.7 1.5 %collective-permute-done.7 = f32[6,2,1,512]{3,2,1,0:T(1,128)S(1)} collective-permute-done((f32[6,2,1,512]{3,2,1,0:T(1,128)S(1)}, f32[6,2,1,512]{3,2,1,0:T(1,128)S(1)}, u32[]{:S(2)}, u32[]{:S(2)}) %collective-permute-start.7) | collective-permute-done | bytes 24608 | tf_op jit(solution)/shard_map/ppermute | solution.py:38
  49.4 1.6 %collective-permute-start.10 = (f32[6,1,18,512]{3,2,1,0:T(8,128)S(1)}, f32[6,1,18,512]{3,2,1,0:T(8,128)S(1)}, u32[]{:S(2)}, u32[]{:S(2)}) collective-permute-start(f32[6,1,18,512]{3,2,1,0:T(8,128)S(1)} %get-tuple-element.18), channel_id=1, source_target_pairs={{0,1},{1,2},{2,3},{3,0},{4,5},{5,6},{6,7},{7,4},{8,9},{9,10},{10,1... | collective-permute-start | bytes 663560 | tf_op jit(solution)/shard_map/ppermute | solution.py:38
  51.0 2.3 %collective-permute-start.9 = (f32[6,1,18,512]{3,2,1,0:T(8,128)S(1)}, f32[6,1,18,512]{3,2,1,0:T(8,128)S(1)}, u32[]{:S(2)}, u32[]{:S(2)}) collective-permute-start(f32[6,1,18,512]{3,2,1,0:T(8,128)S(1)} %get-tuple-element.19), channel_id=1, source_target_pairs={{1,0},{2,1},{3,2},{0,3},{5,4},{6,5},{7,6},{4,7},{9,8},{10,9},{11,1... | collective-permute-start | bytes 663560 | tf_op jit(solution)/shard_map/ppermute | solution.py:39
  54.1 6.9 %collective-permute-done.10 = f32[6,1,18,512]{3,2,1,0:T(8,128)S(1)} collective-permute-done((f32[6,1,18,512]{3,2,1,0:T(8,128)S(1)}, f32[6,1,18,512]{3,2,1,0:T(8,128)S(1)}, u32[]{:S(2)}, u32[]{:S(2)}) %collective-permute-start.10) | collective-permute-done | bytes 221216 | tf_op jit(solution)/shard_map/ppermute | solution.py:38
  61.0 6.1 %collective-permute-done.9 = f32[6,1,18,512]{3,2,1,0:T(8,128)S(1)} collective-permute-done((f32[6,1,18,512]{3,2,1,0:T(8,128)S(1)}, f32[6,1,18,512]{3,2,1,0:T(8,128)S(1)}, u32[]{:S(2)}, u32[]{:S(2)}) %collective-permute-start.9) | collective-permute-done | bytes 221216 | tf_op jit(solution)/shard_map/ppermute | solution.py:39
  71.7 1.4 %maximum_bitcast_fusion = f32[3,2,32,16,16]{4,2,3,1,0:T(8,128)S(1)} fusion(f32[1,2,16,32,16]{4,3,2,1,0:T(8,128)} %stack.55, f32[1,2,16,32,16]{4,3,2,1,0:T(8,128)} %stack.54, f32[1,2,16,32,16]{4,3,2,1,0:T(8,128)S(1)} %stack.53), kind=kLoop, calls=%fused_computation.6 | loop fusion | flops 98304 | bytes 393216 | tf_op jit(solution)/shard_map/transpose | solution.py:94
  73.9 1.5 %gather_fusion.4 = f32[32,3,2,256]{3,2,1,0:T(2,128)} fusion(f32[3,2,32,256]{3,1,2,0:T(2,128)S(1)} %copy.52, s32[1024]{0:T(1024)S(1)} %pad_clamp_fusion.1), kind=kCustom, calls=%fused_computation.4 | custom fusion | bytes 393344 | tf_op jit(solution)/shard_map/gather | solution.py:135
  75.3 3.4 %all-to-all-start.1 = ((f32[3,2,32,256]{3,1,0,2:T(2,128)}), f32[3,2,32,256]{3,1,0,2:T(2,128)S(1)}, u32[]{:S(2)}, u32[]{:S(2)}) async-start(f32[3,2,32,256]{3,1,0,2:T(2,128)} %bitcast.33), calls=%async_computation.1 | async-start | bytes 393216 | tf_op jit(solution)/shard_map/all_to_all | solution.py:138
  79.9 5.0 %all-to-all-done.1 = f32[3,2,32,256]{3,1,0,2:T(2,128)S(1)} async-done(((f32[3,2,32,256]{3,1,0,2:T(2,128)}), f32[3,2,32,256]{3,1,0,2:T(2,128)S(1)}, u32[]{:S(2)}, u32[]{:S(2)}) %all-to-all-start.1) | async-done | bytes 196640 | tf_op jit(solution)/shard_map/all_to_all | solution.py:138
  86.1 3.2 %broadcast_in_dim.20 = f32[3,2,2,32,16,2,16,2]{3,7,6,5,4,2,1,0:T(2,128)S(1)} broadcast(f32[3,2,32,16,16]{2,4,3,1,0:T(8,128)S(1)} %bitcast.70), dimensions={0,1,3,4,6} | broadcast | bytes 1769472 | tf_op jit(solution)/shard_map/broadcast_in_dim | solution.py:140
  89.3 6.3 %add.98 = f32[3,4,32,1024]{2,3,1,0:T(8,128)} add(f32[3,4,32,1024]{2,3,1,0:T(8,128)} %copy.55, f32[3,4,32,1024]{2,3,1,0:T(8,128)S(1)} %bitcast.68) | non-fusion elementwise | flops 393216 | bytes 4718592 | tf_op jit(solution)/shard_map/add | solution.py:144
  95.6 5.5 %copy.56 = f32[3,4,32,1024]{3,2,1,0:T(8,128)} copy(f32[3,4,32,1024]{2,3,1,0:T(8,128)} %add.98) | data formatting | bytes 3145728
  (108 shorter events, 18.3 us)
Async XLA Ops:
  4.4 31.8 %collective-permute-start.6 = (s32[1,1,4,1]{2,3,1,0:T(1,128)S(1)}, s32[1,1,4,1]{2,3,1,0:T(1,128)S(1)}, u32[]{:S(2)}, u32[]{:S(2)}) collective-permute-start(s32[1,1,4,1]{2,3,1,0:T(1,128)S(1)} %get-tuple-element.38), channel_id=1, source_target_pairs={{0,28},{4,24},{8,20},{12,16},{16,12},{20,8},{24,4},{28,0},{1,29},{... | collective-permute-start | bytes 56 | tf_op jit(solution)/shard_map/ppermute | solution.py:26
  7.8 30.4 %collective-permute-start.5 = (s32[1,1,4,1]{2,3,1,0:T(1,128)S(1)}, s32[1,1,4,1]{2,3,1,0:T(1,128)S(1)}, u32[]{:S(2)}, u32[]{:S(2)}) collective-permute-start(s32[1,1,4,1]{2,3,1,0:T(1,128)S(1)} %get-tuple-element.39), channel_id=1, source_target_pairs={{0,24},{4,28},{8,16},{12,20},{16,8},{20,12},{24,0},{28,4},{1,25},{... | collective-permute-start | bytes 56 | tf_op jit(solution)/shard_map/ppermute | solution.py:26
  8.5 29.7 %collective-permute-start.4 = (s32[1,1,4,1]{2,3,1,0:T(1,128)S(1)}, s32[1,1,4,1]{2,3,1,0:T(1,128)S(1)}, u32[]{:S(2)}, u32[]{:S(2)}) collective-permute-start(s32[1,1,4,1]{2,3,1,0:T(1,128)S(1)} %get-tuple-element.40), channel_id=1, source_target_pairs={{0,20},{4,16},{8,28},{12,24},{16,4},{20,0},{24,12},{28,8},{1,21},{... | collective-permute-start | bytes 56 | tf_op jit(solution)/shard_map/ppermute | solution.py:26
  9.8 28.4 %collective-permute-start.3 = (s32[1,1,4,1]{2,3,1,0:T(1,128)S(1)}, s32[1,1,4,1]{2,3,1,0:T(1,128)S(1)}, u32[]{:S(2)}, u32[]{:S(2)}) collective-permute-start(s32[1,1,4,1]{2,3,1,0:T(1,128)S(1)} %get-tuple-element.41), channel_id=1, source_target_pairs={{0,16},{4,20},{8,24},{12,28},{16,0},{20,4},{24,8},{28,12},{1,17},{... | collective-permute-start | bytes 56 | tf_op jit(solution)/shard_map/ppermute | solution.py:26
  10.1 28.1 %collective-permute-start.2 = (s32[1,1,4,1]{2,3,1,0:T(1,128)S(1)}, s32[1,1,4,1]{2,3,1,0:T(1,128)S(1)}, u32[]{:S(2)}, u32[]{:S(2)}) collective-permute-start(s32[1,1,4,1]{2,3,1,0:T(1,128)S(1)} %get-tuple-element.42), channel_id=1, source_target_pairs={{0,12},{4,8},{8,4},{12,0},{16,28},{20,24},{24,20},{28,16},{1,13},{... | collective-permute-start | bytes 56 | tf_op jit(solution)/shard_map/ppermute | solution.py:26
  26.8 15.5 %all-to-all-start = ((f32[3,2,32,256]{3,1,0,2:T(2,128)}), f32[3,2,32,256]{3,1,0,2:T(2,128)S(1)}, u32[]{:S(2)}, u32[]{:S(2)}) async-start(f32[3,2,32,256]{3,1,0,2:T(2,128)} %copy.36), calls=%async_computation | async-start | bytes 393216 | tf_op jit(solution)/shard_map/all_to_all | solution.py:118
  30.3 5.8 %copy-start.12 = (f32[3,2,16,1]{3,2,1,0:T(8,128)}, f32[3,2,16,1]{3,2,1,0:T(8,128)S(1)}, u32[]{:S(2)}) copy-start(f32[3,2,16,1]{3,2,1,0:T(8,128)S(1)} %get-tuple-element.36) | copy-start | bytes 1156
  30.3 5.8 %copy-start.14 = (f32[3,2,16,1]{3,2,1,0:T(8,128)}, f32[3,2,16,1]{3,2,1,0:T(8,128)S(1)}, u32[]{:S(2)}) copy-start(f32[3,2,16,1]{3,2,1,0:T(8,128)S(1)} %get-tuple-element.37) | copy-start | bytes 1156
  30.4 5.7 %copy-start.2 = (f32[3,2,16,511]{3,2,1,0:T(8,128)}, f32[3,2,16,511]{3,2,1,0:T(8,128)S(1)}, u32[]{:S(2)}) copy-start(f32[3,2,16,511]{3,2,1,0:T(8,128)S(1)} %get-tuple-element.35) | copy-start | bytes 588676
  36.2 3.6 %collective-permute-start.1 = (s32[1,1,4,1]{2,3,1,0:T(1,128)S(1)}, s32[1,1,4,1]{2,3,1,0:T(1,128)S(1)}, u32[]{:S(2)}, u32[]{:S(2)}) collective-permute-start(s32[1,1,4,1]{2,3,1,0:T(1,128)S(1)} %get-tuple-element.43), channel_id=1, source_target_pairs={{0,8},{4,12},{8,0},{12,4},{16,24},{20,28},{24,16},{28,20},{1,9},{5... | collective-permute-start | bytes 56 | tf_op jit(solution)/shard_map/ppermute | solution.py:26
  38.2 1.7 %collective-permute-start = (s32[1,1,4,1]{2,3,1,0:T(1,128)S(1)}, s32[1,1,4,1]{2,3,1,0:T(1,128)S(1)}, u32[]{:S(2)}, u32[]{:S(2)}) collective-permute-start(s32[1,1,4,1]{2,3,1,0:T(1,128)S(1)} %get-tuple-element.44), channel_id=1, source_target_pairs={{0,4},{4,0},{8,12},{12,8},{16,20},{20,16},{24,28},{28,24},{1,5},{5... | collective-permute-start | bytes 56 | tf_op jit(solution)/shard_map/ppermute | solution.py:26
  45.0 4.2 %collective-permute-start.7 = (f32[6,2,1,512]{3,2,1,0:T(1,128)S(1)}, f32[6,2,1,512]{3,2,1,0:T(1,128)S(1)}, u32[]{:S(2)}, u32[]{:S(2)}) collective-permute-start(f32[6,2,1,512]{3,2,1,0:T(1,128)S(1)} %get-tuple-element.20), channel_id=1, source_target_pairs={{0,4},{4,8},{8,12},{12,16},{16,20},{20,24},{24,28},{28,0},{1,5},{5... | collective-permute-start | bytes 73736 | tf_op jit(solution)/shard_map/ppermute | solution.py:38
  45.1 4.2 %collective-permute-start.8 = (f32[6,2,1,512]{3,2,1,0:T(1,128)S(1)}, f32[6,2,1,512]{3,2,1,0:T(1,128)S(1)}, u32[]{:S(2)}, u32[]{:S(2)}) collective-permute-start(f32[6,2,1,512]{3,2,1,0:T(1,128)S(1)} %get-tuple-element.21), channel_id=1, source_target_pairs={{4,0},{8,4},{12,8},{16,12},{20,16},{24,20},{28,24},{0,28},{5,1},{9... | collective-permute-start | bytes 73736 | tf_op jit(solution)/shard_map/ppermute | solution.py:39
  49.2 20.1 %copy-start.4 = (f32[6,2,1,512]{3,2,1,0:T(1,128)}, f32[6,2,1,512]{3,2,1,0:T(1,128)S(1)}, u32[]{:S(2)}) copy-start(f32[6,2,1,512]{3,2,1,0:T(1,128)S(1)} %collective-permute-done.7) | copy-start | bytes 73732
  49.3 20.1 %copy-start.6 = (f32[6,2,1,512]{3,2,1,0:T(1,128)}, f32[6,2,1,512]{3,2,1,0:T(1,128)S(1)}, u32[]{:S(2)}) copy-start(f32[6,2,1,512]{3,2,1,0:T(1,128)S(1)} %collective-permute-done.8) | copy-start | bytes 73732
  49.4 11.6 %collective-permute-start.10 = (f32[6,1,18,512]{3,2,1,0:T(8,128)S(1)}, f32[6,1,18,512]{3,2,1,0:T(8,128)S(1)}, u32[]{:S(2)}, u32[]{:S(2)}) collective-permute-start(f32[6,1,18,512]{3,2,1,0:T(8,128)S(1)} %get-tuple-element.18), channel_id=1, source_target_pairs={{0,1},{1,2},{2,3},{3,0},{4,5},{5,6},{6,7},{7,4},{8,9},{9,10},{10,1... | collective-permute-start | bytes 663560 | tf_op jit(solution)/shard_map/ppermute | solution.py:38
  51.0 16.1 %collective-permute-start.9 = (f32[6,1,18,512]{3,2,1,0:T(8,128)S(1)}, f32[6,1,18,512]{3,2,1,0:T(8,128)S(1)}, u32[]{:S(2)}, u32[]{:S(2)}) collective-permute-start(f32[6,1,18,512]{3,2,1,0:T(8,128)S(1)} %get-tuple-element.19), channel_id=1, source_target_pairs={{1,0},{2,1},{3,2},{0,3},{5,4},{6,5},{7,6},{4,7},{9,8},{10,9},{11,1... | collective-permute-start | bytes 663560 | tf_op jit(solution)/shard_map/ppermute | solution.py:39
  73.5 5.4 %copy-start.10 = (f32[3,2,16,512]{3,2,1,0:T(8,128)S(1)}, f32[3,2,16,512]{3,2,1,0:T(8,128)}, u32[]{:S(2)}) copy-start(f32[3,2,16,512]{3,2,1,0:T(8,128)} %fusion.3) | copy-start | bytes 589828
  73.6 5.4 %copy-start.3 = (f32[3,2,16,511]{3,2,1,0:T(8,128)S(1)}, f32[3,2,16,511]{3,2,1,0:T(8,128)}, u32[]{:S(2)}) copy-start(f32[3,2,16,511]{3,2,1,0:T(8,128)} %copy-done.2) | copy-start | bytes 588676
  73.6 5.4 %copy-start.5 = (f32[6,2,1,512]{3,2,1,0:T(1,128)S(1)}, f32[6,2,1,512]{3,2,1,0:T(1,128)}, u32[]{:S(2)}) copy-start(f32[6,2,1,512]{3,2,1,0:T(1,128)} %copy-done.4) | copy-start | bytes 73732
  73.6 5.4 %copy-start.7 = (f32[6,2,1,512]{3,2,1,0:T(1,128)S(1)}, f32[6,2,1,512]{3,2,1,0:T(1,128)}, u32[]{:S(2)}) copy-start(f32[6,2,1,512]{3,2,1,0:T(1,128)} %copy-done.6) | copy-start | bytes 73732
  73.6 5.4 %copy-start.13 = (f32[3,2,16,1]{3,2,1,0:T(8,128)S(1)}, f32[3,2,16,1]{3,2,1,0:T(8,128)}, u32[]{:S(2)}) copy-start(f32[3,2,16,1]{3,2,1,0:T(8,128)} %copy-done.12) | copy-start | bytes 1156
  73.6 5.4 %copy-start.15 = (f32[3,2,16,1]{3,2,1,0:T(8,128)S(1)}, f32[3,2,16,1]{3,2,1,0:T(8,128)}, u32[]{:S(2)}) copy-start(f32[3,2,16,1]{3,2,1,0:T(8,128)} %copy-done.14) | copy-start | bytes 1156
  75.3 9.5 %all-to-all-start.1 = ((f32[3,2,32,256]{3,1,0,2:T(2,128)}), f32[3,2,32,256]{3,1,0,2:T(2,128)S(1)}, u32[]{:S(2)}, u32[]{:S(2)}) async-start(f32[3,2,32,256]{3,1,0,2:T(2,128)} %bitcast.33), calls=%async_computation.1 | async-start | bytes 393216 | tf_op jit(solution)/shard_map/all_to_all | solution.py:138
  (7 other events, 35.3 us)
